TPU v7x, 32 devices: a whole 2x2x4 slice. The times are simulated.
32 devices in a mesh: section: 4 (over y, x), feat: 4 (over z), dp: 2 (over core).
Axes of the slice: x: 2, y: 2, z: 4, core: 2. Of those that a mesh axis runs over, the one named last changes fastest.
Arguments:
- section_outputs: bfloat16 [4, 1024, 4608], P('section', 'dp', 'feat'), may hold values from -6 to 6
- enc_weight: bfloat16 [4608, 16384], P('dp', ('section', 'feat')), may hold values from -0.09375 to 0.09375
- enc_bias: float32 [16384], P(('section', 'feat')), may hold values from -3 to 3
- thresholds: int32 [16384], P(('section', 'feat')), may hold values from 0 to 7
- dec_weight: bfloat16 [16384, 4608], P(('section', 'feat'), 'dp'), may hold values from -0.09375 to 0.09375
- dec_bias: float32 [4608], replicated, may hold values from -3 to 3
- enc_moment: float32 [4608, 16384], P('dp', ('section', 'feat')), may hold values from -2 to 2
- enc_second: float32 [4608, 16384], P('dp', ('section', 'feat')), may hold values from 0.01 to 1
- dec_moment: float32 [16384, 4608], P(('section', 'feat'), 'dp'), may hold values from -2 to 2
- dec_second: float32 [16384, 4608], P(('section', 'feat'), 'dp'), may hold values from 0.01 to 1
Outputs:
- enc_update: bfloat16 [4608, 16384], P('dp', ('section', 'feat'))
- enc_moment_new: float32 [4608, 16384], P('dp', ('section', 'feat'))
- enc_second_new: float32 [4608, 16384], P('dp', ('section', 'feat'))
- dec_update: bfloat16 [16384, 4608], P(('section', 'feat'), 'dp')
- dec_moment_new: float32 [16384, 4608], P(('section', 'feat'), 'dp')
- dec_second_new: float32 [16384, 4608], P(('section', 'feat'), 'dp')
All inputs are finite; a program needn't handle non-finite values.
Results may differ from a plain program's by a relative error of at most 0.0055.
The roundings to bfloat16 on the way count: a program that leaves them out, or rounds other values in their place, can miss the bound.
Values may be sent and summed in bfloat16 or wider, within the bound.
No kernel may reach another device: no remote copies, remote signals or barrier semaphores. Data moves between devices by JAX's collectives and lax.ppermute only.
A program may use at most 256 MiB of HBM per device.

v0:
```python
import math
import jax
import jax.numpy as jnp
from jax import lax
from jax.sharding import PartitionSpec as P

band = 0.1
level_step = 0.25
beta_first = 0.9
beta_second = 0.999
fix_first = 1.0 - (0.9**50) ** 2
fix_second = 1.0 - (0.999**50) ** 2
epsilon = 1e-08


def adam_moves(moment, second, grads):
    moment_new = beta_first * moment + (1.0 - beta_first) * grads
    second_new = beta_second * second + (1.0 - beta_second) * grads * grads
    update = (moment_new / fix_first / (jnp.sqrt(second_new / fix_second) + epsilon)).astype(
        jnp.bfloat16
    )
    return (update, moment_new, second_new)


def on_device(
    section_outputs,
    enc_weight,
    enc_bias,
    thresholds,
    dec_weight,
    dec_bias,
    enc_moment,
    enc_second,
    dec_moment,
    dec_second,
):
    own_part = section_outputs[0].astype(jnp.float32)
    summed = lax.psum(own_part, "section").astype(jnp.bfloat16)
    resid = lax.all_gather(summed, "feat", axis=1, tiled=True)
    tok_rows = resid.shape[0]
    token_total = tok_rows * lax.axis_size("dp")
    columns = resid
    preact = (
        jnp.dot(
            columns,
            lax.all_gather(enc_weight, "dp", axis=0, tiled=True),
            preferred_element_type=jnp.float32,
        )
        + enc_bias
    )
    theta = level_step * (thresholds.astype(jnp.float32) + 1.0)
    opened = jax.nn.sigmoid((preact - theta) / band)
    codes = (preact * opened).astype(jnp.bfloat16)
    dec_full = lax.all_gather(dec_weight, "dp", axis=1, tiled=True)
    groups = lax.axis_size(("section", "feat"))
    position = lax.axis_index(("section", "feat"))
    span = tok_rows // groups
    recon = lax.psum_scatter(
        jnp.dot(codes, dec_full, preferred_element_type=jnp.float32),
        ("section", "feat"),
        scatter_dimension=0,
        tiled=True,
    )
    first = position * span
    target = lax.dynamic_slice_in_dim(resid, first, span, 0).astype(jnp.float32)
    error_part = ((recon + dec_bias - target) / math.sqrt(token_total)).astype(jnp.bfloat16)
    grad_out = lax.all_gather(error_part, ("section", "feat"), axis=0, tiled=True)
    dec_whole = lax.dot_general(
        codes, grad_out, (((0,), (0,)), ((), ())), preferred_element_type=jnp.float32
    )
    dec_grad = lax.psum_scatter(dec_whole, "dp", scatter_dimension=1, tiled=True)
    back = lax.dot_general(
        grad_out, dec_full, (((1,), (1,)), ((), ())), preferred_element_type=jnp.float32
    )
    pre_grad = (back * (opened + preact * opened * (1.0 - opened) / band)).astype(jnp.bfloat16)
    columns = resid
    enc_grad = lax.psum_scatter(
        lax.dot_general(
            columns, pre_grad, (((0,), (0,)), ((), ())), preferred_element_type=jnp.float32
        ),
        "dp",
        scatter_dimension=0,
        tiled=True,
    )
    enc_update, enc_moment_new, enc_second_new = adam_moves(enc_moment, enc_second, enc_grad)
    dec_update, dec_moment_new, dec_second_new = adam_moves(dec_moment, dec_second, dec_grad)
    return (enc_update, enc_moment_new, enc_second_new, dec_update, dec_moment_new, dec_second_new)


def solution(mesh):
    return jax.shard_map(
        on_device,
        mesh=mesh,
        in_specs=(
            P("section", "dp", "feat"),
            P("dp", ("section", "feat")),
            P(("section", "feat")),
            P(("section", "feat")),
            P(("section", "feat"), "dp"),
            P(),
            P("dp", ("section", "feat")),
            P("dp", ("section", "feat")),
            P(("section", "feat"), "dp"),
            P(("section", "feat"), "dp"),
        ),
        out_specs=(
            P("dp", ("section", "feat")),
            P("dp", ("section", "feat")),
            P("dp", ("section", "feat")),
            P(("section", "feat"), "dp"),
            P(("section", "feat"), "dp"),
            P(("section", "feat"), "dp"),
        ),
        check_vma=False,
    )
```

profile of v0, /device:TPU:0, one launch (start us, length us, event | category | flops | bytes accessed | tf_op | source)
XLA Modules:
  0.0 630.2 jit_solution(8954610613970382083)
XLA Ops:
  7.2 0.0 all-gather.5.cloned.1.call-start
  7.2 1.4 bitcast_convert_fusion
  8.6 86.1 %all-reduce.1 = bf16[512,1152]{1,0:T(8,128)(2,1)} all-reduce(f32[512,1152]{1,0:T(8,128)S(1)} %bitcast_convert_fusion), channel_id=1, replica_groups=mesh['section'=4,'feat'=4,'dp'=2] {'section'}, use_global_device_ids=true, to_apply=%region_0.0 | all-reduce | flops 589824 | bytes 3538944 | tf_op jit(solution)/shard_map/psum | solution.py:38
  94.8 0.0 all-gather.5.cloned.1.call-update
  94.8 0.0 copy-start.2
  94.8 0.0 all-gather.7.cloned.1.call-start
  94.9 0.7 all-gather.7.cloned.1.call-update
  95.6 0.0 all-gather.9.cloned.1.call-start
  95.6 0.7 all-gather.9.cloned.1.call-update
  96.3 0.0 reduce-scatter.4.cloned.1.call-start
  96.4 0.0 copy-done.2
  96.4 0.0 copy-start
  96.4 87.7 %all-gather.5.cloned.1.call-done = bf16[512,4608]{1,0:T(8,128)(2,1)} async-done(((bf16[512,1152]{1,0:T(8,128)(2,1)}), bf16[512,4608]{1,0:T(8,128)(2,1)}) %all-gather.5.cloned.1.call-update) | async-done | bytes 4718608 | tf_op jit(solution)/shard_map/all_gather | solution.py:39
  184.1 21.6 %all-gather.7.cloned.1.call-done = bf16[4608,1024]{1,0:T(8,128)(2,1)} async-done(((bf16[2304,1024]{1,0:T(8,128)(2,1)}), bf16[4608,1024]{1,0:T(8,128)(2,1)}) %all-gather.7.cloned.1.call-update) | async-done | bytes 9437200 | tf_op jit(solution)/shard_map/all_gather | solution.py:46
  205.7 9.0 %fusion.15 = f32[512,1024]{1,0:T(8,128)S(1)} fusion(bf16[512,4608]{1,0:T(8,128)(2,1)} %all-gather.5.cloned.1.call-done, bf16[4608,1024]{1,0:T(8,128)(2,1)} %all-gather.7.cloned.1.call-done), kind=kOutput, calls=%fused_computation.24 | convolution fusion | flops 4831838208 | bytes 16252928 | tf_op jit(solution)/shard_map/dot_general | solution.py:44
  214.7 15.4 %all-gather.9.cloned.1.call-done = bf16[1024,4608]{1,0:T(8,128)(2,1)} async-done(((bf16[1024,2304]{1,0:T(8,128)(2,1)}), bf16[1024,4608]{1,0:T(8,128)(2,1)}) %all-gather.9.cloned.1.call-update) | async-done | bytes 9437200 | tf_op jit(solution)/shard_map/all_gather | solution.py:54
  230.1 0.0 copy-done
  230.1 11.3 %fusion.11 = f32[512,4608]{1,0:T(8,128)} fusion(bf16[1024,4608]{1,0:T(8,128)(2,1)} %all-gather.9.cloned.1.call-done, f32[512,1024]{1,0:T(8,128)S(1)} %fusion.15, f32[1024]{0:T(1024)S(1)} %add_multiply_fusion.1, f32[1024]{0:T(1024)S(1)} %copy-done), kind=kOutput, calls=%fused_computation.23 | convolution fusion | flops 4836032512 | bytes 20979712 | tf_op jit(solution)/shard_map/dot_general | solution.py:59
  241.3 0.0 copy-start.1
  241.3 0.0 reduce-scatter.4.cloned.1.call-update
  241.4 0.0 all-gather.11.cloned.1.call-start
  241.4 172.9 %reduce-scatter.4.cloned.1.call-done = f32[32,4608]{1,0:T(8,128)} async-done(((f32[512,4608]{1,0:T(8,128)}), f32[32,4608]{1,0:T(8,128)}) %reduce-scatter.4.cloned.1.call-update) | async-done | bytes 589840 | tf_op jit(solution)/shard_map/reduce_scatter | solution.py:58
  414.3 0.0 copy-done.1
  414.3 1.9 multiply_convert_fusion.1
  416.2 0.0 all-gather.11.cloned.1.call-update
  416.3 0.0 reduce-scatter.6.cloned.1.call-start
  416.3 80.0 %all-gather.11.cloned.1.call-done = bf16[512,4608]{1,0:T(8,128)(2,1)} async-done(((bf16[32,4608]{1,0:T(8,128)(2,1)}), bf16[512,4608]{1,0:T(8,128)(2,1)}) %all-gather.11.cloned.1.call-update) | async-done | bytes 4718608 | tf_op jit(solution)/shard_map/all_gather | solution.py:67
  496.3 19.5 %convolution_bitcast_fusion = f32[4608,1024]{0,1:T(8,128)} fusion(bf16[512,4608]{1,0:T(8,128)(2,1)} %all-gather.5.cloned.1.call-done, f32[512,1024]{1,0:T(8,128)S(1)} %fusion.15, bf16[512,4608]{1,0:T(8,128)(2,1)} %all-gather.11.cloned.1.call-done, bf16[1024,4608]{1,0:T(8,128)(2,1)} %all-gather.9.cloned.1.call-done, f32[1024]{0:T(1024)S(1)} %add_multiply_fusion.1, ...), kind=kOutput, calls=%fused_computation.2 | convolution fusion | flops 9670492160 | bytes 39854080 | tf_op jit(solution)/shard_map/dot_general | solution.py:78
  515.9 0.0 reduce-scatter.6.cloned.1.call-update
  515.9 0.2 reduce-scatter.8.cloned.1.call-start
  516.1 16.0 %fusion.9 = f32[1024,4608]{1,0:T(8,128)} fusion(bf16[512,4608]{1,0:T(8,128)(2,1)} %all-gather.11.cloned.1.call-done, f32[512,1024]{1,0:T(8,128)S(1)} %fusion.15, f32[1024]{0:T(1024)S(1)} %add_multiply_fusion.1, f32[1024]{0:T(1024)S(1)} %copy-done), kind=kOutput, calls=%fused_computation.22 | convolution fusion | flops 4836032512 | bytes 25698304 | tf_op jit(solution)/shard_map/dot_general | solution.py:68
  532.2 0.0 reduce-scatter.8.cloned.1.call-update
  532.2 10.7 %copy.16 = f32[2304,1024]{0,1:T(8,128)} copy(f32[2304,1024]{1,0:T(8,128)} %param.16) | data formatting | bytes 18874368 | tf_op args[6]
  542.9 9.7 %copy.17 = f32[2304,1024]{0,1:T(8,128)} copy(f32[2304,1024]{1,0:T(8,128)} %param.17) | data formatting | bytes 18874368 | tf_op args[7]
  552.6 0.0 reduce-scatter.6.cloned.1.call-done
  552.6 25.6 %divide_convert_fusion.1 = (bf16[2304,1024]{0,1:T(8,128)(2,1)}, f32[2304,1024]{0,1:T(8,128)}, f32[2304,1024]{0,1:T(8,128)}) fusion(f32[2304,1024]{0,1:T(8,128)} %reduce-scatter.6.cloned.1.call-done, f32[2304,1024]{0,1:T(8,128)} %copy.16, f32[2304,1024]{0,1:T(8,128)} %copy.17), kind=kLoop, calls=%fused_computation.7 | loop fusion | flops 28311552 | bytes 51904512 | tf_op jit(solution)/shard_map/convert_element_type | solution.py:19
  578.2 6.6 %copy.18 = bf16[2304,1024]{1,0:T(8,128)(2,1)} copy(bf16[2304,1024]{0,1:T(8,128)(2,1)} %get-tuple-element.15) | data formatting | bytes 9437184
  584.8 9.6 %copy.19 = f32[2304,1024]{1,0:T(8,128)} copy(f32[2304,1024]{0,1:T(8,128)} %get-tuple-element.16) | data formatting | bytes 18874368
  594.4 9.6 %copy.20 = f32[2304,1024]{1,0:T(8,128)} copy(f32[2304,1024]{0,1:T(8,128)} %get-tuple-element.17) | data formatting | bytes 18874368
  604.0 0.0 reduce-scatter.8.cloned.1.call-done
  604.0 19.4 %divide_convert_fusion = (bf16[1024,2304]{1,0:T(8,128)(2,1)}, f32[1024,2304]{1,0:T(8,128)}, f32[1024,2304]{1,0:T(8,128)}) fusion(f32[1024,2304]{1,0:T(8,128)} %reduce-scatter.8.cloned.1.call-done, f32[1024,2304]{1,0:T(8,128)} %param.18, f32[1024,2304]{1,0:T(8,128)} %param.19), kind=kLoop, calls=%fused_computation.5 | loop fusion | flops 28311552 | bytes 51904512 | tf_op jit(solution)/shard_map/convert_element_type | solution.py:19
  (1 shorter events, 0.0 us)
Async XLA Ops:
  7.2 176.9 %all-gather.5.cloned.1.call-start = ((), (), s32[]{:S(2)}) async-start(), calls=%async_computation.3 | async-start | bytes 5898240 | tf_op jit(solution)/shard_map/all_gather | solution.py:39
  94.8 1.5 copy-start.2
  94.8 110.9 %all-gather.7.cloned.1.call-start = ((), (), s32[]{:S(2)}) async-start(), calls=%async_computation.4 | async-start | bytes 14155776 | tf_op jit(solution)/shard_map/all_gather | solution.py:46
  95.6 134.5 %all-gather.9.cloned.1.call-start = ((), (), s32[]{:S(2)}) async-start(), calls=%async_computation.5 | async-start | bytes 14155776 | tf_op jit(solution)/shard_map/all_gather | solution.py:54
  96.3 318.0 %reduce-scatter.4.cloned.1.call-start = ((), (), s32[]{:S(2)}) async-start(), calls=%async_computation.6 | async-start | bytes 10027008 | tf_op jit(solution)/shard_map/reduce_scatter | solution.py:58
  96.4 133.7 %copy-start = (f32[1024]{0:T(1024)S(1)}, f32[1024]{0:T(1024)}, u32[]{:S(2)}) copy-start(f32[1024]{0:T(1024)} %param.12) | copy-start | bytes 12292
  241.3 173.0 %copy-start.1 = (f32[4608]{0:T(1024)S(1)}, f32[4608]{0:T(1024)}, u32[]{:S(2)}) copy-start(f32[4608]{0:T(1024)} %param.15) | copy-start | bytes 55300
  241.4 255.0 %all-gather.11.cloned.1.call-start = ((), (), s32[]{:S(2)}) async-start(), calls=%async_computation.7 | async-start | bytes 5013504 | tf_op jit(solution)/shard_map/all_gather | solution.py:67
  416.3 136.4 %reduce-scatter.6.cloned.1.call-start = ((), (), s32[]{:S(2)}) async-start(), calls=%async_computation.8 | async-start | bytes 28311552 | tf_op jit(solution)/shard_map/reduce_scatter | solution.py:77
  515.9 88.1 %reduce-scatter.8.cloned.1.call-start = ((), (), s32[]{:S(2)}) async-start(), calls=%async_computation.9 | async-start | bytes 28311552 | tf_op jit(solution)/shard_map/reduce_scatter | solution.py:71
Sparse Core Ops, SparseCore 0:
  94.9 89.0 all-gather.4
  185.6 20.0 all-gather.6
  207.3 22.7 all-gather.8
  241.5 172.7 reduce-scatter.3
  417.5 78.8 all-gather.10
  516.0 25.1 reduce-scatter.5
  543.5 27.7 reduce-scatter.7
where the time goes:
time: 631 us; the launch traced here: 630 us
  waiting for transfers between devices  379 us (60%)
  blocking collectives  86.1 us (14%)
  matrix products  55.8 us (9%)
  other arithmetic  48.4 us (8%)
  local copies, waits for them, and re-layouts  46.2 us (7%)
  between operations  14.2 us (2%)
    reduce_scatter x1, waiting for transfers between devices, on_device(): lax.psum_scatter(jnp.dot(codes, dec_full, preferred_element_type=jnp.floa...  173 us
    all_gather x1, waiting for transfers between devices, on_device(): resid = lax.all_gather(summed, 'feat', axis=1, tiled=True)  87.7 us
    psum x1, blocking collectives, on_device(): summed = lax.psum(own_part, 'section').astype(jnp.bfloat16)  86.1 us
    all_gather x1, waiting for transfers between devices, on_device(): lax.all_gather(error_part, ('section', 'feat'), axis=0, tiled=True)  80 us
    unnamed x11, local copies, waits for them, and re-layouts  46.2 us
    convert_element_type x2, other arithmetic, adam_moves(): (moment_new / fix_first / (jnp.sqrt(second_new / fix_second) + epsilon))....  45 us
    all_gather x1, waiting for transfers between devices, on_device(): lax.all_gather(enc_weight, 'dp', axis=0, tiled=True)  21.6 us
    dot_general x1, matrix products, on_device(): lax.dot_general(columns, pre_grad, (((0,), (0,)), ((), ())), preferred_el...  19.5 us
  transfers between devices with their start and end apart: 7, of which 5 were waited for; matrix products, arithmetic and copies ran while one was open for 15% of the time, Pallas kernels for 0%

commit v1 on v0

--- a/solution.py
+++ b/solution.py
@@ -35,7 +35,7 @@
     dec_second,
 ):
     own_part = section_outputs[0].astype(jnp.float32)
-    summed = lax.psum(own_part, "section").astype(jnp.bfloat16)
+    summed = lax.all_gather(own_part, "section").sum(axis=0).astype(jnp.bfloat16)
     resid = lax.all_gather(summed, "feat", axis=1, tiled=True)
     tok_rows = resid.shape[0]
     token_total = tok_rows * lax.axis_size("dp")

time: 631 us -> 607 us (0.962)
  waiting for transfers between devices: 379 us -> 484 us
  blocking collectives: 86.1 us -> 0 us
  local copies, waits for them, and re-layouts: 46.2 us -> 0.04 us
    all_gather x0 -> x1, waiting for transfers between devices: none -> 98.5 us  [on_device(): lax.all_gather(own_part, 'section').sum(axis=0).astype(jnp.bfloat16)]
    psum x1 -> x0, blocking collectives: 86.1 us -> none  [on_device(): summed = lax.psum(own_part, 'section').astype(jnp.bfloat16)]
    unnamed x11 -> x6, local copies, waits for them, and re-layouts: 46.2 us -> 0.04 us
    reduce_scatter x1, waiting for transfers between devices: 0.01 us -> 7.96 us  [on_device(): lax.psum_scatter(lax.dot_general(columns, pre_grad, (((0,), (0,)), ((), (...]
  transfers between devices with their start and end apart: 7 -> 8, of which waited for: 5 -> 8; matrix products, arithmetic and copies ran while one was open for 15% -> 10% of each run, Pallas kernels for 0% -> 0%
where the time goes in v1:
time: 607 us
  waiting for transfers between devices  484 us (80%)
  matrix products  55 us (9%)
  other arithmetic  52.7 us (9%)
  between operations  14.2 us (2%)
    reduce_scatter x1, waiting for transfers between devices, on_device(): lax.psum_scatter(jnp.dot(codes, dec_full, preferred_element_type=jnp.floa...  173 us
    all_gather x1, waiting for transfers between devices, on_device(): lax.all_gather(own_part, 'section').sum(axis=0).astype(jnp.bfloat16)  98.5 us
    all_gather x1, waiting for transfers between devices, on_device(): resid = lax.all_gather(summed, 'feat', axis=1, tiled=True)  92.8 us
    all_gather x1, waiting for transfers between devices, on_device(): lax.all_gather(error_part, ('section', 'feat'), axis=0, tiled=True)  80.2 us
    convert_element_type x2, other arithmetic, adam_moves(): (moment_new / fix_first / (jnp.sqrt(second_new / fix_second) + epsilon))....  42.4 us
    dot_general x1, matrix products, on_device(): lax.dot_general(columns, pre_grad, (((0,), (0,)), ((), ())), preferred_el...  23.3 us
    all_gather x1, waiting for transfers between devices, on_device(): lax.all_gather(enc_weight, 'dp', axis=0, tiled=True)  17 us
    all_gather x1, waiting for transfers between devices, on_device(): dec_full = lax.all_gather(dec_weight, 'dp', axis=1, tiled=True)  12.5 us
  transfers between devices with their start and end apart: 8, of which 8 were waited for; matrix products, arithmetic and copies ran while one was open for 10% of the time, Pallas kernels for 0%

profile of v1, /device:TPU:0, one launch (start us, length us, event | category | flops | bytes accessed | tf_op | source)
XLA Modules:
  0.0 606.9 jit_solution(7311320905511182496)
XLA Ops:
  7.2 0.0 all-gather.6.cloned.1.call-start
  7.2 2.8 convert_element_type.28
  10.0 0.0 all-gather.6.cloned.1.call-update
  10.1 0.0 all-gather.10.cloned.1.call-start
  10.1 0.7 all-gather.10.cloned.1.call-update
  10.8 0.0 all-gather.8.cloned.1.call-start
  10.9 98.5 %all-gather.6.cloned.1.call-done = f32[4,512,1152]{2,1,0:T(8,128)} async-done(((f32[1,512,1152]{2,1,0:T(8,128)}), f32[4,512,1152]{2,1,0:T(8,128)}) %all-gather.6.cloned.1.call-update) | async-done | bytes 9437200 | tf_op jit(solution)/shard_map/all_gather | solution.py:38
  109.3 5.6 reduce_sum.9
  114.9 0.0 copy-start.2
  114.9 0.0 all-gather.8.cloned.1.call-update
  114.9 0.0 all-gather.12.cloned.1.call-start
  115.0 0.5 all-gather.12.cloned.1.call-update
  115.5 0.0 reduce-scatter.4.cloned.1.call-start
  115.6 0.0 copy-done.2
  115.6 0.0 copy-start
  115.6 17.0 %all-gather.10.cloned.1.call-done = bf16[4608,1024]{1,0:T(8,128)(2,1)} async-done(((bf16[2304,1024]{1,0:T(8,128)(2,1)}), bf16[4608,1024]{1,0:T(8,128)(2,1)}) %all-gather.10.cloned.1.call-update) | async-done | bytes 9437200 | tf_op jit(solution)/shard_map/all_gather | solution.py:46
  132.6 92.8 %all-gather.8.cloned.1.call-done = bf16[512,4608]{1,0:T(8,128)(2,1)} async-done(((bf16[512,1152]{1,0:T(8,128)(2,1)}), bf16[512,4608]{1,0:T(8,128)(2,1)}) %all-gather.8.cloned.1.call-update) | async-done | bytes 4718608 | tf_op jit(solution)/shard_map/all_gather | solution.py:39
  225.3 9.0 %fusion.16 = f32[512,1024]{1,0:T(8,128)S(1)} fusion(bf16[512,4608]{1,0:T(8,128)(2,1)} %all-gather.8.cloned.1.call-done, bf16[4608,1024]{1,0:T(8,128)(2,1)} %all-gather.10.cloned.1.call-done), kind=kOutput, calls=%fused_computation.23 | convolution fusion | flops 4831838208 | bytes 16252928 | tf_op jit(solution)/shard_map/dot_general | solution.py:44
  234.3 12.5 %all-gather.12.cloned.1.call-done = bf16[1024,4608]{1,0:T(8,128)(2,1)} async-done(((bf16[1024,2304]{1,0:T(8,128)(2,1)}), bf16[1024,4608]{1,0:T(8,128)(2,1)}) %all-gather.12.cloned.1.call-update) | async-done | bytes 9437200 | tf_op jit(solution)/shard_map/all_gather | solution.py:54
  246.8 0.0 copy-done
  246.8 11.2 %fusion.12 = f32[512,4608]{1,0:T(8,128)} fusion(bf16[1024,4608]{1,0:T(8,128)(2,1)} %all-gather.12.cloned.1.call-done, f32[512,1024]{1,0:T(8,128)S(1)} %fusion.16, f32[1024]{0:T(1024)S(1)} %add_multiply_fusion.1, f32[1024]{0:T(1024)S(1)} %copy-done), kind=kOutput, calls=%fused_computation.22 | convolution fusion | flops 4836032512 | bytes 20979712 | tf_op jit(solution)/shard_map/dot_general | solution.py:59
  258.0 0.0 copy-start.1
  258.0 0.0 reduce-scatter.4.cloned.1.call-update
  258.0 0.0 all-gather.14.cloned.1.call-start
  258.1 172.6 %reduce-scatter.4.cloned.1.call-done = f32[32,4608]{1,0:T(8,128)} async-done(((f32[512,4608]{1,0:T(8,128)}), f32[32,4608]{1,0:T(8,128)}) %reduce-scatter.4.cloned.1.call-update) | async-done | bytes 589840 | tf_op jit(solution)/shard_map/reduce_scatter | solution.py:58
  430.7 0.0 copy-done.1
  430.7 1.9 multiply_convert_fusion.1
  432.6 0.0 all-gather.14.cloned.1.call-update
  432.6 0.0 reduce-scatter.8.cloned.1.call-start
  432.7 80.2 %all-gather.14.cloned.1.call-done = bf16[512,4608]{1,0:T(8,128)(2,1)} async-done(((bf16[32,4608]{1,0:T(8,128)(2,1)}), bf16[512,4608]{1,0:T(8,128)(2,1)}) %all-gather.14.cloned.1.call-update) | async-done | bytes 4718608 | tf_op jit(solution)/shard_map/all_gather | solution.py:67
  512.9 11.5 %fusion.10 = f32[1024,4608]{1,0:T(8,128)} fusion(bf16[512,4608]{1,0:T(8,128)(2,1)} %all-gather.14.cloned.1.call-done, f32[512,1024]{1,0:T(8,128)S(1)} %fusion.16, f32[1024]{0:T(1024)S(1)} %add_multiply_fusion.1, f32[1024]{0:T(1024)S(1)} %copy-done), kind=kOutput, calls=%fused_computation.21 | convolution fusion | flops 4836032512 | bytes 25698304 | tf_op jit(solution)/shard_map/dot_general | solution.py:68
  524.4 0.0 reduce-scatter.8.cloned.1.call-update
  524.4 0.2 reduce-scatter.6.cloned.1.call-start
  524.7 23.3 %fusion.3 = f32[4608,1024]{1,0:T(8,128)} fusion(bf16[512,4608]{1,0:T(8,128)(2,1)} %all-gather.8.cloned.1.call-done, f32[512,1024]{1,0:T(8,128)S(1)} %fusion.16, bf16[512,4608]{1,0:T(8,128)(2,1)} %all-gather.14.cloned.1.call-done, bf16[1024,4608]{1,0:T(8,128)(2,1)} %all-gather.12.cloned.1.call-done, f32[1024]{0:T(1024)S(1)} %add_multiply_fusion.1, ...), kind=kOutput, calls=%fused_computation.12 | convolution fusion | flops 9670492160 | bytes 39854080 | tf_op jit(solution)/shard_map/dot_general | solution.py:78
  547.9 0.0 reduce-scatter.6.cloned.1.call-update
  547.9 1.8 reduce-scatter.8.cloned.1.call-done
  549.7 22.2 %divide_convert_fusion = (bf16[1024,2304]{1,0:T(8,128)(2,1)}, f32[1024,2304]{1,0:T(8,128)}, f32[1024,2304]{1,0:T(8,128)}) fusion(f32[1024,2304]{1,0:T(8,128)} %reduce-scatter.8.cloned.1.call-done, f32[1024,2304]{1,0:T(8,128)} %param.18, f32[1024,2304]{1,0:T(8,128)} %param.19), kind=kLoop, calls=%fused_computation.4 | loop fusion | flops 28311552 | bytes 51904512 | tf_op jit(solution)/shard_map/convert_element_type | solution.py:19
  572.0 8.0 %reduce-scatter.6.cloned.1.call-done = f32[2304,1024]{1,0:T(8,128)} async-done(((f32[4608,1024]{1,0:T(8,128)}), f32[2304,1024]{1,0:T(8,128)}) %reduce-scatter.6.cloned.1.call-update) | async-done | bytes 9437200 | tf_op jit(solution)/shard_map/reduce_scatter | solution.py:77
  579.9 20.1 %divide_convert_fusion.1 = (bf16[2304,1024]{1,0:T(8,128)(2,1)}, f32[2304,1024]{1,0:T(8,128)}, f32[2304,1024]{1,0:T(8,128)}) fusion(f32[2304,1024]{1,0:T(8,128)} %reduce-scatter.6.cloned.1.call-done, f32[2304,1024]{1,0:T(8,128)} %param.16, f32[2304,1024]{1,0:T(8,128)} %param.17), kind=kLoop, calls=%fused_computation.6 | loop fusion | flops 28311552 | bytes 51904512 | tf_op jit(solution)/shard_map/convert_element_type | solution.py:19
  (1 shorter events, 0.0 us)
Async XLA Ops:
  7.2 102.2 %all-gather.6.cloned.1.call-start = ((), (), s32[]{:S(2)}) async-start(), calls=%async_computation.3 | async-start | bytes 11796480 | tf_op jit(solution)/shard_map/all_gather | solution.py:38
  10.1 122.5 %all-gather.10.cloned.1.call-start = ((), (), s32[]{:S(2)}) async-start(), calls=%async_computation.5 | async-start | bytes 14155776 | tf_op jit(solution)/shard_map/all_gather | solution.py:46
  10.8 214.5 %all-gather.8.cloned.1.call-start = ((), (), s32[]{:S(2)}) async-start(), calls=%async_computation.4 | async-start | bytes 5898240 | tf_op jit(solution)/shard_map/all_gather | solution.py:39
  114.9 0.7 copy-start.2
  114.9 131.8 %all-gather.12.cloned.1.call-start = ((), (), s32[]{:S(2)}) async-start(), calls=%async_computation.6 | async-start | bytes 14155776 | tf_op jit(solution)/shard_map/all_gather | solution.py:54
  115.5 315.1 %reduce-scatter.4.cloned.1.call-start = ((), (), s32[]{:S(2)}) async-start(), calls=%async_computation.7 | async-start | bytes 10027008 | tf_op jit(solution)/shard_map/reduce_scatter | solution.py:58
  115.6 131.2 %copy-start = (f32[1024]{0:T(1024)S(1)}, f32[1024]{0:T(1024)}, u32[]{:S(2)}) copy-start(f32[1024]{0:T(1024)} %param.12) | copy-start | bytes 12292
  258.0 172.6 %copy-start.1 = (f32[4608]{0:T(1024)S(1)}, f32[4608]{0:T(1024)}, u32[]{:S(2)}) copy-start(f32[4608]{0:T(1024)} %param.15) | copy-start | bytes 55300
  258.0 254.8 %all-gather.14.cloned.1.call-start = ((), (), s32[]{:S(2)}) async-start(), calls=%async_computation.8 | async-start | bytes 5013504 | tf_op jit(solution)/shard_map/all_gather | solution.py:67
  432.6 117.1 %reduce-scatter.8.cloned.1.call-start = ((), (), s32[]{:S(2)}) async-start(), calls=%async_computation.10 | async-start | bytes 28311552 | tf_op jit(solution)/shard_map/reduce_scatter | solution.py:71
  524.4 55.5 %reduce-scatter.6.cloned.1.call-start = ((), (), s32[]{:S(2)}) async-start(), calls=%async_computation.9 | async-start | bytes 28311552 | tf_op jit(solution)/shard_map/reduce_scatter | solution.py:77
Sparse Core Ops, SparseCore 0:
  10.4 98.9 all-gather.5
  110.9 21.6 all-gather.9
  134.7 90.5 all-gather.7
  226.7 19.9 all-gather.11
  258.2 172.4 reduce-scatter.3
  433.8 78.9 all-gather.13
  524.5 25.1 reduce-scatter.7
  552.0 27.8 reduce-scatter.5
